TPU v7x, 32 devices: a whole 2x2x4 slice. The times are simulated.
32 devices in a mesh: seq: 8 (over y, x, core), tile: 4 (over z).
Axes of the slice: x: 2, y: 2, z: 4, core: 2. Of those that a mesh axis runs over, the one named last changes fastest.
Arguments:
- inputs: bfloat16 [8, 13, 256, 1024], P('seq', None, 'tile'), may hold values from -6 to 6
- actions: int32 [8, 13], P('seq'), may hold values from 0 to 7
- segments: int32 [8, 13], P('seq'), may hold values from 0 to 3, never falling along the last dimension, each value on 1 to 6 neighbouring positions
- cotangent: bfloat16 [8, 13, 256, 1024], P('seq', None, 'tile'), may hold values from -6 to 6
- action_table: bfloat16 [8, 1024], P(None, 'seq'), may hold values from -6 to 6
- spatial_inward: bfloat16 [1024, 3072], P('seq'), may hold values from -0.1875 to 0.1875
- spatial_outward: bfloat16 [1024, 1024], P('seq'), may hold values from -3 to 3
- temporal_inward: bfloat16 [1024, 3072], P('seq'), may hold values from -0.1875 to 0.1875
- temporal_outward: bfloat16 [1024, 1024], P('seq'), may hold values from -0.375 to 0.375
- expand_weight: bfloat16 [1024, 4096], P('seq'), may hold values from -0.1875 to 0.1875
- contract_weight: bfloat16 [4096, 1024], P('seq'), may hold values from -0.09375 to 0.09375
- expand_bias: bfloat16 [4096], P('seq'), may hold values from -3 to 3
- contract_bias: bfloat16 [1024], P('seq'), may hold values from -3 to 3
- norm_gain: bfloat16 [3, 1024], P(None, 'seq'), may hold values from 0.5 to 1.5
- norm_shift: bfloat16 [3, 1024], P(None, 'seq'), may hold values from -3 to 3
Outputs:
- outputs: bfloat16 [8, 13, 256, 1024], P('seq', None, 'tile')
- input_grad: bfloat16 [8, 13, 256, 1024], P('seq', None, 'tile')
- action_table_grad: float32 [8, 1024], P(None, 'seq')
- spatial_inward_grad: float32 [1024, 3072], P('seq')
- spatial_outward_grad: float32 [1024, 1024], P('seq')
- temporal_inward_grad: float32 [1024, 3072], P('seq')
- temporal_outward_grad: float32 [1024, 1024], P('seq')
- expand_weight_grad: float32 [1024, 4096], P('seq')
- contract_weight_grad: float32 [4096, 1024], P('seq')
- expand_bias_grad: float32 [4096], P('seq')
- contract_bias_grad: float32 [1024], P('seq')
- norm_gain_grad: float32 [3, 1024], P(None, 'seq')
- norm_shift_grad: float32 [3, 1024], P(None, 'seq')
Inputs may be any that keep to these rules, and one draw needn't show every extreme that they name: Within a packed sequence the segment ids never fall from frame to frame; each sequence holds 4 segments of at most 6 frames each.
All inputs are finite; a program needn't handle non-finite values.
Results may differ from a plain program's by a relative error of at most 0.018.
Values may be sent and summed in bfloat16 or wider, within the bound.
No kernel may reach another device: no remote copies, remote signals or barrier semaphores. Data moves between devices by JAX's collectives and lax.ppermute only.
A program may use at most 320 MiB of HBM per device.

v0:
```python
import jax
import jax.numpy as jnp
from jax import lax
from jax.sharding import PartitionSpec as P

HEAD = 64
epsilon = 1e-05
masked_score = -1e30


def gelu_tanh(hidden):
    return jax.nn.gelu(hidden, approximate=True)


def norm_parts(hidden, gain_row, shift_row):
    centre = jnp.mean(hidden, axis=-1, keepdims=True)
    centred = hidden - centre
    spread = jnp.mean(centred * centred, axis=-1, keepdims=True)
    inverse = lax.rsqrt(spread + epsilon)
    normed = centred * inverse
    return ((normed * gain_row + shift_row).astype(jnp.bfloat16), normed, inverse)


def norm_back(upstream, normed, inverse, gain_row):
    scaled = upstream * gain_row
    mean_first = jnp.mean(scaled, axis=-1, keepdims=True)
    mean_second = jnp.mean(scaled * normed, axis=-1, keepdims=True)
    grad_back = inverse * (scaled - mean_first - normed * mean_second)
    return (grad_back, jnp.sum(upstream * normed, axis=0), jnp.sum(upstream, axis=0))


def soft_rows(scores):
    row_top = jnp.max(scores, axis=-1, keepdims=True)
    powered = jnp.exp(scores - row_top)
    row_total = jnp.sum(powered, axis=-1, keepdims=True)
    return (powered / row_total, row_top + jnp.log(row_total))


def score_grads(softmaxed, grad_soft):
    inner_sum = jnp.sum(grad_soft * softmaxed, axis=-1, keepdims=True)
    return (softmaxed * (grad_soft - inner_sum)).astype(jnp.bfloat16)


def body(
    inputs,
    actions,
    segments,
    cotangent,
    action_table,
    spatial_inward,
    spatial_outward,
    temporal_inward,
    temporal_outward,
    expand_weight,
    contract_weight,
    expand_bias,
    contract_bias,
    norm_gain,
    norm_shift,
):
    (
        table_full,
        space_in,
        space_out,
        time_in,
        time_out,
        expand_full,
        contract_full,
        expand_shift,
        contract_shift,
        gain_full,
        shift_full,
    ) = (
        lax.all_gather(action_table, "seq", axis=1, tiled=True),
        lax.all_gather(spatial_inward, "seq", axis=0, tiled=True),
        lax.all_gather(spatial_outward, "seq", axis=0, tiled=True),
        lax.all_gather(temporal_inward, "seq", axis=0, tiled=True),
        lax.all_gather(temporal_outward, "seq", axis=0, tiled=True),
        lax.all_gather(expand_weight, "seq", axis=0, tiled=True),
        lax.all_gather(contract_weight, "seq", axis=0, tiled=True),
        lax.all_gather(expand_bias, "seq", axis=0, tiled=True),
        lax.all_gather(contract_bias, "seq", axis=0, tiled=True),
        lax.all_gather(norm_gain, "seq", axis=1, tiled=True),
        lax.all_gather(norm_shift, "seq", axis=1, tiled=True),
    )
    packed_count, frames, tile_cells, model_width = inputs.shape
    row_count = packed_count * frames * tile_cells
    head_count = model_width // HEAD
    score_scale = HEAD ** (-0.5)
    frame_width = tile_cells * lax.axis_size("tile")
    gain_rows = gain_full.astype(jnp.float32)
    shift_rows = shift_full.astype(jnp.float32)
    f32 = jnp.float32
    bf16 = jnp.bfloat16
    onehot = (
        actions[:, :, None] == jnp.arange(table_full.shape[0], dtype=jnp.int32)[None, None, :]
    ).astype(bf16)
    embedded = jnp.einsum("sfa,ad->sfd", onehot, table_full, preferred_element_type=f32)
    embed_sum = (inputs.astype(f32) + embedded[:, :, None, :]).reshape(row_count, model_width)
    normed_one, unit_one, inverse_one = norm_parts(embed_sum, gain_rows[0], shift_rows[0])
    projected = jnp.dot(normed_one, space_in, preferred_element_type=f32).astype(bf16)
    space_query = projected[:, :model_width].reshape(
        packed_count, frames, tile_cells, head_count, HEAD
    )
    own_keys = projected[:, model_width : 2 * model_width].reshape(
        packed_count, frames, tile_cells, model_width
    )
    own_values = projected[:, 2 * model_width :].reshape(
        packed_count, frames, tile_cells, model_width
    )
    frame_keys, frame_values = (
        lax.all_gather(own_keys, "tile", axis=2, tiled=True),
        lax.all_gather(own_values, "tile", axis=2, tiled=True),
    )
    key_heads = frame_keys.reshape(packed_count, frames, frame_width, head_count, HEAD)
    value_heads = frame_values.reshape(packed_count, frames, frame_width, head_count, HEAD)

    def space_scores():
        return (
            jnp.einsum("sfqhd,sfkhd->sfhqk", space_query, key_heads, preferred_element_type=f32)
            * score_scale
        )

    space_soft, space_lse = soft_rows(space_scores())
    space_mixed = jnp.einsum(
        "sfhqk,sfkhd->sfqhd", space_soft.astype(bf16), value_heads, preferred_element_type=f32
    )
    space_mixed = space_mixed.astype(bf16).reshape(row_count, model_width)
    space_sum = embed_sum + jnp.dot(space_mixed, space_out, preferred_element_type=f32)
    normed_two, unit_two, inverse_two = norm_parts(space_sum, gain_rows[1], shift_rows[1])
    time_proj = jnp.dot(normed_two, time_in, preferred_element_type=f32).astype(bf16)
    time_proj = time_proj.reshape(packed_count, frames, tile_cells, 3, head_count, HEAD)
    time_query = time_proj[:, :, :, 0]
    time_keys = time_proj[:, :, :, 1]
    time_values = time_proj[:, :, :, 2]
    frame_index = jnp.arange(frames, dtype=jnp.int32)
    allowed = (frame_index[None, None, :] <= frame_index[None, :, None]) & (
        segments[:, None, :] == segments[:, :, None]
    )
    allowed_heads = allowed[:, None, None, :, :]

    def time_scores():
        raw_scores = (
            jnp.einsum("sfphd,sgphd->sphfg", time_query, time_keys, preferred_element_type=f32)
            * score_scale
        )
        return jnp.where(allowed_heads, raw_scores, masked_score)

    time_soft, time_lse = soft_rows(time_scores())
    time_mixed = jnp.einsum(
        "sphfg,sgphd->sfphd", time_soft.astype(bf16), time_values, preferred_element_type=f32
    )
    time_mixed = time_mixed.astype(bf16).reshape(row_count, model_width)
    time_sum = space_sum + jnp.dot(time_mixed, time_out, preferred_element_type=f32)
    normed_three, unit_three, inverse_three = norm_parts(time_sum, gain_rows[2], shift_rows[2])
    expanded = jnp.dot(normed_three, expand_full, preferred_element_type=f32) + expand_shift.astype(
        f32
    )
    activated, gelu_pull = jax.vjp(gelu_tanh, expanded)
    activated_low = activated.astype(bf16)
    block_out = (
        time_sum
        + jnp.dot(activated_low, contract_full, preferred_element_type=f32)
        + contract_shift.astype(f32)
    )
    outputs = block_out.astype(bf16).reshape(inputs.shape)
    upstream = cotangent.astype(f32).reshape(row_count, model_width)
    grad_contract_shift = jnp.sum(upstream, axis=0)
    upstream_low = upstream.astype(bf16)
    grad_contract = jnp.einsum("rf,rd->fd", activated_low, upstream_low, preferred_element_type=f32)
    grad_activated = jnp.einsum(
        "rd,fd->rf", upstream_low, contract_full, preferred_element_type=f32
    )
    grad_expanded = gelu_pull(grad_activated)[0].astype(bf16)
    grad_expand_shift = jnp.sum(grad_expanded.astype(f32), axis=0)
    grad_expand = jnp.einsum("rd,rf->df", normed_three, grad_expanded, preferred_element_type=f32)
    grad_normed_three = jnp.einsum(
        "rf,df->rd", grad_expanded, expand_full, preferred_element_type=f32
    )
    back_three, gain_three, shift_three = norm_back(
        grad_normed_three, unit_three, inverse_three, gain_rows[2]
    )
    grad_time_sum = upstream + back_three
    time_low = grad_time_sum.astype(bf16)
    grad_time_out = jnp.einsum("rd,re->de", time_mixed, time_low, preferred_element_type=f32)
    grad_time_mixed = jnp.einsum(
        "re,de->rd", time_low, time_out, preferred_element_type=f32
    ).astype(bf16)
    grad_time_mixed = grad_time_mixed.reshape(packed_count, frames, tile_cells, head_count, HEAD)
    time_again = jnp.exp(time_scores() - time_lse)
    grad_time_values = jnp.einsum(
        "sphfg,sfphd->sgphd", time_again.astype(bf16), grad_time_mixed, preferred_element_type=f32
    )
    grad_time_soft = jnp.einsum(
        "sfphd,sgphd->sphfg", grad_time_mixed, time_values, preferred_element_type=f32
    )
    grad_time_scores = score_grads(time_again, grad_time_soft)
    grad_time_query = (
        jnp.einsum("sphfg,sgphd->sfphd", grad_time_scores, time_keys, preferred_element_type=f32)
        * score_scale
    )
    grad_time_keys = (
        jnp.einsum("sphfg,sfphd->sgphd", grad_time_scores, time_query, preferred_element_type=f32)
        * score_scale
    )
    grad_time_proj = jnp.stack([grad_time_query, grad_time_keys, grad_time_values], axis=3).astype(
        bf16
    )
    grad_time_proj = grad_time_proj.reshape(row_count, 3 * model_width)
    grad_time_in = jnp.einsum("rd,re->de", normed_two, grad_time_proj, preferred_element_type=f32)
    grad_normed_two = jnp.einsum("re,de->rd", grad_time_proj, time_in, preferred_element_type=f32)
    back_two, gain_two, shift_two = norm_back(grad_normed_two, unit_two, inverse_two, gain_rows[1])
    grad_space_sum = grad_time_sum + back_two
    space_low = grad_space_sum.astype(bf16)
    grad_space_out = jnp.einsum("rd,re->de", space_mixed, space_low, preferred_element_type=f32)
    grad_space_mixed = jnp.einsum(
        "re,de->rd", space_low, space_out, preferred_element_type=f32
    ).astype(bf16)
    grad_space_mixed = grad_space_mixed.reshape(packed_count, frames, tile_cells, head_count, HEAD)
    space_again = jnp.exp(space_scores() - space_lse)
    grad_space_soft = jnp.einsum(
        "sfqhd,sfkhd->sfhqk", grad_space_mixed, value_heads, preferred_element_type=f32
    )
    grad_space_scores = score_grads(space_again, grad_space_soft)
    grad_space_query = (
        jnp.einsum("sfhqk,sfkhd->sfqhd", grad_space_scores, key_heads, preferred_element_type=f32)
        * score_scale
    )
    grad_frame_values = jnp.einsum(
        "sfhqk,sfqhd->sfkhd", space_again.astype(bf16), grad_space_mixed, preferred_element_type=f32
    )
    grad_frame_keys = (
        jnp.einsum("sfhqk,sfqhd->sfkhd", grad_space_scores, space_query, preferred_element_type=f32)
        * score_scale
    )
    grad_frame_keys = grad_frame_keys.reshape(packed_count, frames, frame_width, model_width)
    grad_frame_values = grad_frame_values.reshape(packed_count, frames, frame_width, model_width)
    own_grad_keys, own_grad_values = (
        lax.psum_scatter(
            grad_frame_keys.astype(jnp.bfloat16), "tile", scatter_dimension=2, tiled=True
        ).astype(jnp.float32),
        lax.psum_scatter(
            grad_frame_values.astype(jnp.bfloat16), "tile", scatter_dimension=2, tiled=True
        ).astype(jnp.float32),
    )
    grad_space_proj = jnp.concatenate(
        [
            grad_space_query.reshape(row_count, model_width),
            own_grad_keys.reshape(row_count, model_width),
            own_grad_values.reshape(row_count, model_width),
        ],
        axis=1,
    ).astype(bf16)
    grad_space_in = jnp.einsum("rd,re->de", normed_one, grad_space_proj, preferred_element_type=f32)
    grad_normed_one = jnp.einsum("re,de->rd", grad_space_proj, space_in, preferred_element_type=f32)
    back_one, gain_one, shift_one = norm_back(grad_normed_one, unit_one, inverse_one, gain_rows[0])
    grad_embed_sum = grad_space_sum + back_one
    input_grad = grad_embed_sum.astype(bf16).reshape(inputs.shape)
    per_frame = jnp.sum(
        grad_embed_sum.reshape(packed_count, frames, tile_cells, model_width), axis=2
    )
    grad_table = jnp.einsum(
        "sfa,sfd->ad", onehot.astype(f32), per_frame, precision=lax.Precision.HIGHEST
    )
    grad_gains = jnp.stack([gain_one, gain_two, gain_three], axis=0)
    grad_shifts = jnp.stack([shift_one, shift_two, shift_three], axis=0)
    local_grads = (
        grad_table,
        grad_space_in,
        grad_space_out,
        grad_time_in,
        grad_time_out,
        grad_expand,
        grad_contract,
        grad_expand_shift,
        grad_contract_shift,
        grad_gains,
        grad_shifts,
    )
    shards = (
        lax.psum_scatter(
            local_grads[0].astype(jnp.bfloat16), "seq", scatter_dimension=1, tiled=True
        ).astype(jnp.float32),
        lax.psum_scatter(
            local_grads[1].astype(jnp.bfloat16), "seq", scatter_dimension=0, tiled=True
        ).astype(jnp.float32),
        lax.psum_scatter(
            local_grads[2].astype(jnp.bfloat16), "seq", scatter_dimension=0, tiled=True
        ).astype(jnp.float32),
        lax.psum_scatter(
            local_grads[3].astype(jnp.bfloat16), "seq", scatter_dimension=0, tiled=True
        ).astype(jnp.float32),
        lax.psum_scatter(
            local_grads[4].astype(jnp.bfloat16), "seq", scatter_dimension=0, tiled=True
        ).astype(jnp.float32),
        lax.psum_scatter(
            local_grads[5].astype(jnp.bfloat16), "seq", scatter_dimension=0, tiled=True
        ).astype(jnp.float32),
        lax.psum_scatter(
            local_grads[6].astype(jnp.bfloat16), "seq", scatter_dimension=0, tiled=True
        ).astype(jnp.float32),
        lax.psum_scatter(
            local_grads[7].astype(jnp.bfloat16), "seq", scatter_dimension=0, tiled=True
        ).astype(jnp.float32),
        lax.psum_scatter(
            local_grads[8].astype(jnp.bfloat16), "seq", scatter_dimension=0, tiled=True
        ).astype(jnp.float32),
        lax.psum_scatter(
            local_grads[9].astype(jnp.bfloat16), "seq", scatter_dimension=1, tiled=True
        ).astype(jnp.float32),
        lax.psum_scatter(
            local_grads[10].astype(jnp.bfloat16), "seq", scatter_dimension=1, tiled=True
        ).astype(jnp.float32),
    )
    summed = (
        lax.psum(shards[0].astype(jnp.bfloat16), "tile").astype(jnp.float32),
        lax.psum(shards[1].astype(jnp.bfloat16), "tile").astype(jnp.float32),
        lax.psum(shards[2].astype(jnp.bfloat16), "tile").astype(jnp.float32),
        lax.psum(shards[3].astype(jnp.bfloat16), "tile").astype(jnp.float32),
        lax.psum(shards[4].astype(jnp.bfloat16), "tile").astype(jnp.float32),
        lax.psum(shards[5].astype(jnp.bfloat16), "tile").astype(jnp.float32),
        lax.psum(shards[6].astype(jnp.bfloat16), "tile").astype(jnp.float32),
        lax.psum(shards[7].astype(jnp.bfloat16), "tile").astype(jnp.float32),
        lax.psum(shards[8].astype(jnp.bfloat16), "tile").astype(jnp.float32),
        lax.psum(shards[9].astype(jnp.bfloat16), "tile").astype(jnp.float32),
        lax.psum(shards[10].astype(jnp.bfloat16), "tile").astype(jnp.float32),
    )
    return (
        outputs,
        input_grad,
        summed[0],
        summed[1],
        summed[2],
        summed[3],
        summed[4],
        summed[5],
        summed[6],
        summed[7],
        summed[8],
        summed[9],
        summed[10],
    )


def solution(mesh):
    placed = (
        P("seq", None, "tile", None),
        P("seq", None),
        P("seq", None),
        P("seq", None, "tile", None),
        P(None, "seq"),
        P("seq", None),
        P("seq", None),
        P("seq", None),
        P("seq", None),
        P("seq", None),
        P("seq", None),
        P("seq"),
        P("seq"),
        P(None, "seq"),
        P(None, "seq"),
    )
    return jax.shard_map(
        body,
        mesh=mesh,
        in_specs=placed,
        out_specs=(
            P("seq", None, "tile", None),
            P("seq", None, "tile", None),
            P(None, "seq"),
            P("seq", None),
            P("seq", None),
            P("seq", None),
            P("seq", None),
            P("seq", None),
            P("seq", None),
            P("seq"),
            P("seq"),
            P(None, "seq"),
            P(None, "seq"),
        ),
        check_vma=False,
    )
```

profile of v0, /device:TPU:0, one launch (start us, length us, event | category | flops | bytes accessed | tf_op | source)
XLA Modules:
  0.0 1583.9 jit_solution(6852255820230631596)
XLA Ops:
  8.0 10.5 all_gather.39
  42.3 15.9 %all-gather.11.cloned.1.call-done = bf16[1024,3072]{1,0:T(8,128)(2,1)} async-done(((bf16[128,3072]{1,0:T(8,128)(2,1)}), bf16[1024,3072]{1,0:T(8,128)(2,1)}) %all-gather.11.cloned.1.call-update) | async-done | bytes 6291472 | tf_op jit(solution)/shard_map/all_gather | solution.py:75
  91.1 101.7 %all-gather.15.cloned.1.call-done = bf16[1,13,256,1024]{3,2,1,0:T(8,128)(2,1)} async-done(((bf16[1,13,64,1024]{3,2,1,0:T(8,128)(2,1)}), bf16[1,13,256,1024]{3,2,1,0:T(8,128)(2,1)}) %all-gather.15.cloned.1.call-update) | async-done | bytes 6815760 | tf_op jit(solution)/shard_map/all_gather | solution.py:112
  203.2 114.0 %all-gather.13.cloned.1.call-done = bf16[1,13,256,1024]{3,2,1,0:T(8,128)(2,1)} async-done(((bf16[1,13,64,1024]{3,2,1,0:T(8,128)(2,1)}), bf16[1,13,256,1024]{3,2,1,0:T(8,128)(2,1)}) %all-gather.13.cloned.1.call-update) | async-done | bytes 6815760 | tf_op jit(solution)/shard_map/all_gather | solution.py:113
  365.9 26.4 %all-gather.19.cloned.1.call-done = bf16[1024,3072]{1,0:T(8,128)(2,1)} async-done(((bf16[128,3072]{1,0:T(8,128)(2,1)}), bf16[1024,3072]{1,0:T(8,128)(2,1)}) %all-gather.19.cloned.1.call-update) | async-done | bytes 6291472 | tf_op jit(solution)/shard_map/all_gather | solution.py:77
  392.3 10.5 convolution_convert_fusion.5
  402.8 13.3 reshape.501
  450.2 28.1 %all-gather.23.cloned.1.call-done = bf16[1024,4096]{1,0:T(8,128)(2,1)} async-done(((bf16[128,4096]{1,0:T(8,128)(2,1)}), bf16[1024,4096]{1,0:T(8,128)(2,1)}) %all-gather.23.cloned.1.call-update) | async-done | bytes 8388624 | tf_op jit(solution)/shard_map/all_gather | solution.py:79
  478.3 13.9 fusion.51
  492.1 42.4 %all-gather.25.cloned.1.call-done = bf16[4096,1024]{1,0:T(8,128)(2,1)} async-done(((bf16[512,1024]{1,0:T(8,128)(2,1)}), bf16[4096,1024]{1,0:T(8,128)(2,1)}) %all-gather.25.cloned.1.call-update) | async-done | bytes 8388624 | tf_op jit(solution)/shard_map/all_gather | solution.py:80
  534.6 22.3 %fusion.52 = (bf16[4096]{0:T(1024)(128)(2,1)}, bf16[832,4096]{1,0:T(8,128)(2,1)}) fusion(f32[832,4096]{1,0:T(8,128)} %fusion.51, f32[4096]{0:T(1024)S(1)} %bitcast.176, bf16[832,1024]{1,0:T(8,128)(2,1)} %bitcast.155, bf16[4096,1024]{1,0:T(8,128)(2,1)} %all-gather.25.cloned.1.call-done), kind=kOutput, calls=%fused_computation.128 | convolution fusion | flops 7054290944 | bytes 30564352 | tf_op jit(solution)/shard_map/rd,fd->rf/dot_general | solution.py:171
  556.9 13.3 multiply_reduce_fusion.3
  590.0 12.0 multiply_reduce_fusion.2
  625.6 13.8 convert_element_type.256
  682.3 13.3 multiply_reduce_fusion
  733.3 12.1 convolution_convert_fusion.3
  746.9 16.9 %convolution_convert_fusion = bf16[4096,1024]{1,0:T(8,128)(2,1)} fusion(bf16[832,1024]{1,0:T(8,128)(2,1)S(1)} %bitcast.156, f32[832,4096]{1,0:T(8,128)} %fusion.51, f32[4096]{0:T(1024)S(1)} %bitcast.177), kind=kOutput, calls=%fused_computation.28 | convolution fusion | flops 7017594880 | bytes 23740416 | tf_op jit(solution)/shard_map/rf,rd->fd/dot_general | solution.py:170
  765.8 14.6 convolution_convert_fusion.1
  801.7 121.9 %reduce-scatter.18.cloned.1.call-done = bf16[1,13,64,1024]{3,2,1,0:T(8,128)(2,1)} async-done(((bf16[1,13,256,1024]{3,2,1,0:T(8,128)(2,1)}), bf16[1,13,64,1024]{3,2,1,0:T(8,128)(2,1)}) %reduce-scatter.18.cloned.1.call-update) | async-done | bytes 1703952 | tf_op jit(solution)/shard_map/reduce_scatter | solution.py:239
  923.6 11.4 convolution_convert_fusion.4
  937.2 12.5 multiply_reduce_fusion.5
  969.2 45.3 %reduce-scatter.24.cloned.1.call-done = bf16[128,1024]{1,0:T(8,128)(2,1)} async-done(((bf16[1024,1024]{1,0:T(8,128)(2,1)}), bf16[128,1024]{1,0:T(8,128)(2,1)}) %reduce-scatter.24.cloned.1.call-update) | async-done | bytes 262160 | tf_op jit(solution)/shard_map/reduce_scatter | solution.py:287
  1014.6 65.2 %reduce-scatter.26.cloned.1.call-done = bf16[128,3072]{1,0:T(8,128)(2,1)} async-done(((bf16[1024,3072]{1,0:T(8,128)(2,1)}), bf16[128,3072]{1,0:T(8,128)(2,1)}) %reduce-scatter.26.cloned.1.call-update) | async-done | bytes 786448 | tf_op jit(solution)/shard_map/reduce_scatter | solution.py:290
  1079.8 75.0 %reduce-scatter.32.cloned.1.call-done = bf16[512,1024]{1,0:T(8,128)(2,1)} async-done(((bf16[4096,1024]{1,0:T(8,128)(2,1)}), bf16[512,1024]{1,0:T(8,128)(2,1)}) %reduce-scatter.32.cloned.1.call-update) | async-done | bytes 1048592 | tf_op jit(solution)/shard_map/reduce_scatter | solution.py:299
  1154.8 74.6 %reduce-scatter.30.cloned.1.call-done = bf16[128,4096]{1,0:T(8,128)(2,1)} async-done(((bf16[1024,4096]{1,0:T(8,128)(2,1)}), bf16[128,4096]{1,0:T(8,128)(2,1)}) %reduce-scatter.30.cloned.1.call-update) | async-done | bytes 1048592 | tf_op jit(solution)/shard_map/reduce_scatter | solution.py:296
  1229.4 65.4 %reduce-scatter.22.cloned.1.call-done = bf16[128,3072]{1,0:T(8,128)(2,1)} async-done(((bf16[1024,3072]{1,0:T(8,128)(2,1)}), bf16[128,3072]{1,0:T(8,128)(2,1)}) %reduce-scatter.22.cloned.1.call-update) | async-done | bytes 786448 | tf_op jit(solution)/shard_map/reduce_scatter | solution.py:284
  1307.1 23.7 %all-reduce.2 = (bf16[4096]{0:T(1024)(128)(2,1)S(1)}, bf16[1024]{0:T(1024)(128)(2,1)S(1)}) all-reduce(bf16[4096]{0:T(1024)(128)(2,1)S(1)} %copy-done.54, bf16[1024]{0:T(1024)(128)(2,1)S(1)} %reduce_sum.249), channel_id=11, replica_groups=mesh['seq'=8,'tile'=4] {'seq'}, use_global_device_ids=true, to_apply=%region_36.37.clone | all-reduce | flops 5120 | bytes 20480
  1330.9 15.2 add_convert_fusion
  1346.9 22.3 %reduce-scatter.36.cloned.1.call-done = bf16[128,3]{1,0:T(8,128)(2,1)} async-done(((bf16[1024,3]{1,0:T(8,128)(2,1)}), bf16[128,3]{1,0:T(8,128)(2,1)}) %reduce-scatter.36.cloned.1.call-update) | async-done | bytes 784
  1370.0 36.5 %reduce-scatter.34.cloned.1.call-done = bf16[128,8]{1,0:T(8,128)(2,1)} async-done(((bf16[1024,8]{1,0:T(8,128)(2,1)}), bf16[128,8]{1,0:T(8,128)(2,1)}) %reduce-scatter.34.cloned.1.call-update) | async-done | bytes 2064
  1407.3 12.0 all-reduce.3
  1422.1 144.1 %all-reduce.7.cloned.1.call-done = (bf16[128,3072]{1,0:T(8,128)(2,1)}, bf16[128,1024]{1,0:T(8,128)(2,1)}, bf16[128,3072]{1,0:T(8,128)(2,1)}, bf16[128,1024]{1,0:...) async-done(((bf16[128,3072]{1,0:T(8,128)(2,1)}, bf16[128,1024]{1,0:T(8,128)(2,1)}, bf16[128,3072]{1,0:T(8,128)(2,1)}, bf16[128,1024]{1,0:T(8,128)(2,1)}, ...) | async-done | bytes 4194320 | tf_op jit(solution)/shard_map/psum | solution.py:317
  (291 shorter events, 347.4 us)
Async XLA Ops:
  7.2 51.0 %all-gather.11.cloned.1.call-start = ((), (), s32[]{:S(2)}) async-start(), calls=%async_computation.11 | async-start | bytes 7077888 | tf_op jit(solution)/shard_map/all_gather | solution.py:75
  7.9 184.9 %all-gather.15.cloned.1.call-start = ((), (), s32[]{:S(2)}) async-start(), calls=%async_computation.13 | async-start | bytes 8519680 | tf_op jit(solution)/shard_map/all_gather | solution.py:112
  40.5 351.8 %copy-start.46 = (f32[1,1024]{1,0:T(1,128)}, f32[1,1024]{1,0:T(1,128)S(1)}, u32[]{:S(2)}) copy-start(f32[1,1024]{1,0:T(1,128)S(1)} %get-tuple-element.51) | copy-start | bytes 12292
  40.5 529.7 %copy-start.50 = (f32[1,1024]{1,0:T(1,128)}, f32[1,1024]{1,0:T(1,128)S(1)}, u32[]{:S(2)}) copy-start(f32[1,1024]{1,0:T(1,128)S(1)} %get-tuple-element.50) | copy-start | bytes 12292
  40.5 351.8 %copy-start.57 = (f32[1,1024]{1,0:T(1,128)}, f32[1,1024]{1,0:T(1,128)S(1)}, u32[]{:S(2)}) copy-start(f32[1,1024]{1,0:T(1,128)S(1)} %get-tuple-element.54) | copy-start | bytes 12292
  40.5 437.7 %copy-start.55 = (f32[1,1024]{1,0:T(1,128)}, f32[1,1024]{1,0:T(1,128)S(1)}, u32[]{:S(2)}) copy-start(f32[1,1024]{1,0:T(1,128)S(1)} %get-tuple-element.53) | copy-start | bytes 12292
  68.8 248.4 %all-gather.13.cloned.1.call-start = ((), (), s32[]{:S(2)}) async-start(), calls=%async_computation.12 | async-start | bytes 8519680 | tf_op jit(solution)/shard_map/all_gather | solution.py:113
  69.5 290.1 %all-gather.17.cloned.1.call-start = ((), (), s32[]{:S(2)}) async-start(), calls=%async_computation.14 | async-start | bytes 2359296 | tf_op jit(solution)/shard_map/all_gather | solution.py:76
  70.1 322.2 %all-gather.19.cloned.1.call-start = ((), (), s32[]{:S(2)}) async-start(), calls=%async_computation.15 | async-start | bytes 7077888 | tf_op jit(solution)/shard_map/all_gather | solution.py:77
  70.7 371.8 %all-gather.21.cloned.1.call-start = ((), (), s32[]{:S(2)}) async-start(), calls=%async_computation.16 | async-start | bytes 2359296 | tf_op jit(solution)/shard_map/all_gather | solution.py:78
  71.2 407.0 %all-gather.23.cloned.1.call-start = ((), (), s32[]{:S(2)}) async-start(), calls=%async_computation.17 | async-start | bytes 9437184 | tf_op jit(solution)/shard_map/all_gather | solution.py:79
  72.0 462.6 %all-gather.25.cloned.1.call-start = ((), (), s32[]{:S(2)}) async-start(), calls=%async_computation.18 | async-start | bytes 9437184 | tf_op jit(solution)/shard_map/all_gather | solution.py:80
  72.7 729.0 %reduce-scatter.20.cloned.1.call-start = ((), (), s32[]{:S(2)}) async-start(), calls=%async_computation.20 | async-start | bytes 8519680 | tf_op jit(solution)/shard_map/reduce_scatter | solution.py:242
  81.9 452.6 %copy-start.52 = (f32[8,1,512]{2,1,0:T(1,128)}, f32[8,1,512]{2,1,0:T(1,128)S(1)}, u32[]{:S(2)}) copy-start(f32[8,1,512]{2,1,0:T(1,128)S(1)} %convert_element_type.288) | copy-start | bytes 49156
  447.7 122.6 %copy-start.15 = (f32[832,1024]{1,0:T(8,128)}, f32[832,1024]{1,0:T(8,128)S(1)}, u32[]{:S(2)}) copy-start(f32[832,1024]{1,0:T(8,128)S(1)} %get-tuple-element.63) | copy-start | bytes 10223620
  447.7 122.6 %copy-start.40 = (f32[832]{0:T(1024)}, f32[832]{0:T(1024)S(1)}, u32[]{:S(2)}) copy-start(f32[832]{0:T(1024)S(1)} %broadcast_multiply_fusion.7) | copy-start | bytes 9988
  448.2 122.1 %copy-start.48 = (f32[832]{0:T(1024)}, f32[832]{0:T(1024)S(1)}, u32[]{:S(2)}) copy-start(f32[832]{0:T(1024)S(1)} %add_rsqrt_fusion.1) | copy-start | bytes 9988
  682.3 241.3 %reduce-scatter.18.cloned.1.call-start = ((), (), s32[]{:S(2)}) async-start(), calls=%async_computation.19 | async-start | bytes 8519680 | tf_op jit(solution)/shard_map/reduce_scatter | solution.py:239
  721.4 247.8 %reduce-scatter.28.cloned.1.call-start = ((), (), s32[]{:S(2)}) async-start(), calls=%async_computation.24 | async-start | bytes 2359296 | tf_op jit(solution)/shard_map/reduce_scatter | solution.py:293
  727.8 286.8 %reduce-scatter.24.cloned.1.call-start = ((), (), s32[]{:S(2)}) async-start(), calls=%async_computation.22 | async-start | bytes 2359296 | tf_op jit(solution)/shard_map/reduce_scatter | solution.py:287
  733.3 346.5 %reduce-scatter.26.cloned.1.call-start = ((), (), s32[]{:S(2)}) async-start(), calls=%async_computation.23 | async-start | bytes 7077888 | tf_op jit(solution)/shard_map/reduce_scatter | solution.py:290
  745.5 409.3 %reduce-scatter.32.cloned.1.call-start = ((), (), s32[]{:S(2)}) async-start(), calls=%async_computation.26 | async-start | bytes 9437184 | tf_op jit(solution)/shard_map/reduce_scatter | solution.py:299
  763.9 465.5 %reduce-scatter.30.cloned.1.call-start = ((), (), s32[]{:S(2)}) async-start(), calls=%async_computation.25 | async-start | bytes 9437184 | tf_op jit(solution)/shard_map/reduce_scatter | solution.py:296
  780.4 514.3 %reduce-scatter.22.cloned.1.call-start = ((), (), s32[]{:S(2)}) async-start(), calls=%async_computation.21 | async-start | bytes 7077888 | tf_op jit(solution)/shard_map/reduce_scatter | solution.py:284
  935.1 411.0 %reduce-scatter.38.cloned.1.call-start = ((), (), s32[]{:S(2)}) async-start(), calls=%async_computation.29 | async-start | bytes 294912
  950.6 418.6 %reduce-scatter.36.cloned.1.call-start = ((), (), s32[]{:S(2)}) async-start(), calls=%async_computation.28 | async-start | bytes 294912
  956.7 338.1 %copy-start.69 = (u32[32]{0:T(128)S(1)}, u32[32]{0:T(128)}, u32[]{:S(2)}) copy-start(u32[32]{0:T(128)} %constant.48) | copy-start | bytes 388
  959.1 339.3 %copy-start.66 = (bf16[128]{0:T(256)(128)(2,1)S(1)}, bf16[128]{0:T(256)(128)(2,1)}, u32[]{:S(2)}) copy-start(bf16[128]{0:T(256)(128)(2,1)} %param.27) | copy-start | bytes 772
  959.2 347.9 %copy-start.54 = (bf16[4096]{0:T(1024)(128)(2,1)S(1)}, bf16[4096]{0:T(1024)(128)(2,1)}, u32[]{:S(2)}) copy-start(bf16[4096]{0:T(1024)(128)(2,1)} %get-tuple-element.38) | copy-start | bytes 24580
  959.2 371.8 %copy-start.17 = (f32[832,1024]{1,0:T(8,128)S(1)}, f32[832,1024]{1,0:T(8,128)}, u32[]{:S(2)}) copy-start(f32[832,1024]{1,0:T(8,128)} %copy-done.15) | copy-start | bytes 10223620
  959.2 447.3 %reduce-scatter.34.cloned.1.call-start = ((), (), s32[]{:S(2)}) async-start(), calls=%async_computation.27 | async-start | bytes 294912
  960.4 605.8 %all-reduce.7.cloned.1.call-start = ((), (), s32[]{:S(2)}) async-start(), calls=%async_computation.30 | async-start | bytes 8388608 | tf_op jit(solution)/shard_map/psum | solution.py:317
  (58 other events, 514.6 us)
Sparse Core Ops, SparseCore 0:
  9.9 48.2 all-gather.10
  68.9 123.9 all-gather.14
  195.0 122.0 all-gather.12
  318.9 26.0 all-gather.16
  346.7 45.5 all-gather.18
  394.0 27.8 all-gather.20
  423.8 54.3 all-gather.22
  480.1 54.3 all-gather.24
  682.4 119.2 reduce-scatter.19
  803.8 119.7 reduce-scatter.17
  927.5 41.6 reduce-scatter.27
  973.3 41.2 reduce-scatter.23
  1018.0 61.7 reduce-scatter.25
  1083.5 71.2 reduce-scatter.31
  1158.1 71.2 reduce-scatter.29
  1233.0 61.7 reduce-scatter.21
  1298.2 33.6 reduce-scatter.37
  1335.6 33.5 reduce-scatter.35
  1372.8 33.6 reduce-scatter.33
  1409.4 156.7 all-reduce.6
where the time goes:
time: 1590 us; the launch traced here: 1580 us
  waiting for transfers between devices  996 us (63%)
  matrix products  276 us (17%)
  local copies, waits for them, and re-layouts  149 us (9%)
  blocking collectives  80.6 us (5%)
  other arithmetic  64.8 us (4%)
  between operations  16.6 us (1%)
    psum x1, waiting for transfers between devices, body(): lax.psum(shards[1].astype(jnp.bfloat16), 'tile').astype(jnp.float32)  144 us
    reduce_scatter x1, waiting for transfers between devices, body(): lax.psum_scatter(grad_frame_keys.astype(jnp.bfloat16), 'tile', scatter_di...  122 us
    all_gather x1, waiting for transfers between devices, body(): lax.all_gather(own_values, 'tile', axis=2, tiled=True)  114 us
    all_gather x1, waiting for transfers between devices, body(): lax.all_gather(own_keys, 'tile', axis=2, tiled=True)  102 us
    reduce_scatter x1, waiting for transfers between devices, body(): lax.psum_scatter(local_grads[6].astype(jnp.bfloat16), 'seq', scatter_dime...  75 us
    reduce_scatter x1, waiting for transfers between devices, body(): lax.psum_scatter(local_grads[5].astype(jnp.bfloat16), 'seq', scatter_dime...  74.6 us
    reduce_scatter x1, waiting for transfers between devices, body(): lax.psum_scatter(local_grads[1].astype(jnp.bfloat16), 'seq', scatter_dime...  65.4 us
    reduce_scatter x1, waiting for transfers between devices, body(): lax.psum_scatter(local_grads[3].astype(jnp.bfloat16), 'seq', scatter_dime...  65.2 us
  transfers between devices with their start and end apart: 20, of which 17 were waited for; matrix products, arithmetic and copies ran while one was open for 20% of the time, Pallas kernels for 0%

commit v1 on v0

--- a/solution.py
+++ b/solution.py
@@ -6,6 +6,18 @@
 HEAD = 64
 epsilon = 1e-05
 masked_score = -1e30
+
+
+def collect(x, axis, dim):
+    ways, here, lap = (lax.axis_size(axis), lax.axis_index(axis), x.shape[dim])
+    line, have = (x, 1)
+    while have < ways:
+        line = jnp.concatenate(
+            [line, lax.ppermute(line, axis, [(d, (d - have) % ways) for d in range(ways)])],
+            axis=dim,
+        )
+        have = 2 * have
+    return jnp.roll(line, here * lap, axis=dim)
 
 
 def gelu_tanh(hidden):
@@ -77,7 +89,7 @@
         lax.all_gather(temporal_inward, "seq", axis=0, tiled=True),
         lax.all_gather(temporal_outward, "seq", axis=0, tiled=True),
         lax.all_gather(expand_weight, "seq", axis=0, tiled=True),
-        lax.all_gather(contract_weight, "seq", axis=0, tiled=True),
+        collect(contract_weight, "seq", 0),
         lax.all_gather(expand_bias, "seq", axis=0, tiled=True),
         lax.all_gather(contract_bias, "seq", axis=0, tiled=True),
         lax.all_gather(norm_gain, "seq", axis=1, tiled=True),

time: 1590 us -> 1550 us (0.975)
  waiting for transfers between devices: 996 us -> 842 us
  blocking collectives: 80.6 us -> 167 us
  local copies, waits for them, and re-layouts: 149 us -> 165 us
    all_gather x1, waiting for transfers between devices: 114 us -> 0.01 us  [body(): lax.all_gather(own_values, 'tile', axis=2, tiled=True)]
    all_gather x1, blocking collectives: 9.03 us -> 95.4 us  [body(): lax.all_gather(expand_bias, 'seq', axis=0, tiled=True)]
    ppermute x0 -> x3, waiting for transfers between devices: none -> 58.8 us  [collect(): lax.ppermute(line, axis, [(d, (d - have) % ways) for d in range(ways)])]
    all_gather x1, waiting for transfers between devices: 102 us -> 48.4 us  [body(): lax.all_gather(own_keys, 'tile', axis=2, tiled=True)]
    all_gather x1 -> x0, waiting for transfers between devices: 42.4 us -> none  [body(): lax.all_gather(contract_weight, 'seq', axis=0, tiled=True)]
    reduce_scatter x1, waiting for transfers between devices: 8.78 us -> 45.5 us  [body(): lax.psum_scatter(local_grads[4].astype(jnp.bfloat16), 'seq', scatter_dime...]
    reduce_scatter x1, waiting for transfers between devices: 45.3 us -> 8.69 us  [body(): lax.psum_scatter(local_grads[2].astype(jnp.bfloat16), 'seq', scatter_dime...]
    unnamed x23 -> x22, waiting for transfers between devices: 63.3 us -> 60.8 us
  transfers between devices with their start and end apart: 20 -> 22, of which waited for: 17 -> 17; matrix products, arithmetic and copies ran while one was open for 20% -> 20% of each run, Pallas kernels for 0% -> 0%
where the time goes in v1:
time: 1550 us; the launch traced here: 1540 us
  waiting for transfers between devices  842 us (54%)
  matrix products  276 us (18%)
  blocking collectives  167 us (11%)
  local copies, waits for them, and re-layouts  165 us (11%)
  other arithmetic  69.2 us (4%)
  between operations  16.5 us (1%)
    psum x1, waiting for transfers between devices, body(): lax.psum(shards[1].astype(jnp.bfloat16), 'tile').astype(jnp.float32)  144 us
    reduce_scatter x1, waiting for transfers between devices, body(): lax.psum_scatter(grad_frame_keys.astype(jnp.bfloat16), 'tile', scatter_di...  122 us
    all_gather x1, blocking collectives, body(): lax.all_gather(expand_bias, 'seq', axis=0, tiled=True)  95.4 us
    reduce_scatter x1, waiting for transfers between devices, body(): lax.psum_scatter(local_grads[5].astype(jnp.bfloat16), 'seq', scatter_dime...  75.2 us
    reduce_scatter x1, waiting for transfers between devices, body(): lax.psum_scatter(local_grads[6].astype(jnp.bfloat16), 'seq', scatter_dime...  74.6 us
    reduce_scatter x1, waiting for transfers between devices, body(): lax.psum_scatter(local_grads[1].astype(jnp.bfloat16), 'seq', scatter_dime...  65.4 us
    reduce_scatter x1, waiting for transfers between devices, body(): lax.psum_scatter(local_grads[3].astype(jnp.bfloat16), 'seq', scatter_dime...  65 us
    unnamed x22, waiting for transfers between devices  60.8 us
  transfers between devices with their start and end apart: 22, of which 17 were waited for; matrix products, arithmetic and copies ran while one was open for 20% of the time, Pallas kernels for 0%

profile of v1, /device:TPU:0, one launch (start us, length us, event | category | flops | bytes accessed | tf_op | source)
XLA Modules:
  0.0 1542.4 jit_solution(11276677049070969725)
XLA Ops:
  42.3 15.9 %all-gather.10.cloned.1.call-done = bf16[1024,3072]{1,0:T(8,128)(2,1)} async-done(((bf16[128,3072]{1,0:T(8,128)(2,1)}), bf16[1024,3072]{1,0:T(8,128)(2,1)}) %all-gather.10.cloned.1.call-update) | async-done | bytes 6291472 | tf_op jit(solution)/shard_map/all_gather | solution.py:87
  72.1 12.3 collective-permute-done
  88.3 46.5 %collective-permute-done.1 = bf16[1024,1024]{1,0:T(8,128)(2,1)S(1)} collective-permute-done((bf16[1024,1024]{1,0:T(8,128)(2,1)}, bf16[1024,1024]{1,0:T(8,128)(2,1)S(1)}, u32[]{:S(2)}, u32[]{:S(2)}) %collective-permute-start.1) | collective-permute-done | bytes 2097184 | tf_op jit(solution)/shard_map/ppermute | solution.py:16
  140.6 95.4 %all-gather = bf16[8,1,512]{2,1,0:T(2,128)(2,1)S(1)} all-gather(bf16[1,1,512]{2,1,0:T(2,128)(2,1)S(1)} %reshape.516), channel_id=1, replica_groups=mesh['seq'=8,'tile'=4] {'seq'}, dimensions={0}, use_global_device_ids=true | all-gather | bytes 9216 | tf_op jit(solution)/shard_map/all_gather | solution.py:93
  268.8 48.4 %all-gather.14.cloned.1.call-done = bf16[1,13,256,1024]{3,2,1,0:T(8,128)(2,1)} async-done(((bf16[1,13,64,1024]{3,2,1,0:T(8,128)(2,1)}), bf16[1,13,256,1024]{3,2,1,0:T(8,128)(2,1)}) %all-gather.14.cloned.1.call-update) | async-done | bytes 6815760 | tf_op jit(solution)/shard_map/all_gather | solution.py:124
  366.1 26.2 %all-gather.18.cloned.1.call-done = bf16[1024,3072]{1,0:T(8,128)(2,1)} async-done(((bf16[128,3072]{1,0:T(8,128)(2,1)}), bf16[1024,3072]{1,0:T(8,128)(2,1)}) %all-gather.18.cloned.1.call-update) | async-done | bytes 6291472 | tf_op jit(solution)/shard_map/all_gather | solution.py:89
  392.3 10.5 convolution_convert_fusion.5
  402.8 13.3 reshape.501
  449.6 28.7 %all-gather.22.cloned.1.call-done = bf16[1024,4096]{1,0:T(8,128)(2,1)} async-done(((bf16[128,4096]{1,0:T(8,128)(2,1)}), bf16[1024,4096]{1,0:T(8,128)(2,1)}) %all-gather.22.cloned.1.call-update) | async-done | bytes 8388624 | tf_op jit(solution)/shard_map/all_gather | solution.py:91
  478.3 14.1 fusion.64
  492.4 25.0 %fusion.72 = (bf16[4096]{0:T(1024)(128)(2,1)}, bf16[832,4096]{1,0:T(8,128)(2,1)}) fusion(f32[832,4096]{1,0:T(8,128)} %fusion.64, f32[4096]{0:T(1024)S(1)} %bitcast.187, bf16[832,1024]{1,0:T(8,128)(2,1)S(1)} %bitcast.166, bf16[8192,1024]{1,0:T(8,128)(2,1)} %copy-done.39, s32[]{:T(128)S(6)} %select_n.21), kind=kOutput, calls=%fused_computation.156 | convolution fusion | flops 7054290944 | bytes 30564356 | tf_op jit(solution)/shard_map/rd,fd->rf/dot_general | solution.py:183
  517.4 11.4 multiply_reduce_fusion.3
  548.8 11.9 multiply_reduce_fusion.2
  584.3 13.8 convert_element_type.256
  640.9 13.3 multiply_reduce_fusion
  693.7 11.5 convolution_convert_fusion.3
  707.2 14.4 convolution_convert_fusion.1
  723.0 17.0 %convolution_convert_fusion = bf16[4096,1024]{1,0:T(8,128)(2,1)} fusion(bf16[832,1024]{1,0:T(8,128)(2,1)S(1)} %bitcast.167, f32[832,4096]{1,0:T(8,128)} %fusion.64, f32[4096]{0:T(1024)S(1)} %bitcast.188), kind=kOutput, calls=%fused_computation.33 | convolution fusion | flops 7017594880 | bytes 23740416 | tf_op jit(solution)/shard_map/rf,rd->fd/dot_general | solution.py:182
  760.2 122.1 %reduce-scatter.18.cloned.1.call-done = bf16[1,13,64,1024]{3,2,1,0:T(8,128)(2,1)} async-done(((bf16[1,13,256,1024]{3,2,1,0:T(8,128)(2,1)}), bf16[1,13,64,1024]{3,2,1,0:T(8,128)(2,1)}) %reduce-scatter.18.cloned.1.call-update) | async-done | bytes 1703952 | tf_op jit(solution)/shard_map/reduce_scatter | solution.py:251
  882.3 11.4 convolution_convert_fusion.4
  895.9 12.4 multiply_reduce_fusion.5
  927.8 45.5 %reduce-scatter.28.cloned.1.call-done = bf16[128,1024]{1,0:T(8,128)(2,1)} async-done(((bf16[1024,1024]{1,0:T(8,128)(2,1)}), bf16[128,1024]{1,0:T(8,128)(2,1)}) %reduce-scatter.28.cloned.1.call-update) | async-done | bytes 262160 | tf_op jit(solution)/shard_map/reduce_scatter | solution.py:305
  973.3 65.0 %reduce-scatter.26.cloned.1.call-done = bf16[128,3072]{1,0:T(8,128)(2,1)} async-done(((bf16[1024,3072]{1,0:T(8,128)(2,1)}), bf16[128,3072]{1,0:T(8,128)(2,1)}) %reduce-scatter.26.cloned.1.call-update) | async-done | bytes 786448 | tf_op jit(solution)/shard_map/reduce_scatter | solution.py:302
  1038.3 75.2 %reduce-scatter.30.cloned.1.call-done = bf16[128,4096]{1,0:T(8,128)(2,1)} async-done(((bf16[1024,4096]{1,0:T(8,128)(2,1)}), bf16[128,4096]{1,0:T(8,128)(2,1)}) %reduce-scatter.30.cloned.1.call-update) | async-done | bytes 1048592 | tf_op jit(solution)/shard_map/reduce_scatter | solution.py:308
  1113.5 74.6 %reduce-scatter.32.cloned.1.call-done = bf16[512,1024]{1,0:T(8,128)(2,1)} async-done(((bf16[4096,1024]{1,0:T(8,128)(2,1)}), bf16[512,1024]{1,0:T(8,128)(2,1)}) %reduce-scatter.32.cloned.1.call-update) | async-done | bytes 1048592 | tf_op jit(solution)/shard_map/reduce_scatter | solution.py:311
  1188.1 65.4 %reduce-scatter.22.cloned.1.call-done = bf16[128,3072]{1,0:T(8,128)(2,1)} async-done(((bf16[1024,3072]{1,0:T(8,128)(2,1)}), bf16[128,3072]{1,0:T(8,128)(2,1)}) %reduce-scatter.22.cloned.1.call-update) | async-done | bytes 786448 | tf_op jit(solution)/shard_map/reduce_scatter | solution.py:296
  1265.8 24.0 %all-reduce.2 = (bf16[4096]{0:T(1024)(128)(2,1)S(1)}, bf16[1024]{0:T(1024)(128)(2,1)S(1)}) all-reduce(bf16[4096]{0:T(1024)(128)(2,1)S(1)} %copy-done.54, bf16[1024]{0:T(1024)(128)(2,1)S(1)} %reduce_sum.249), channel_id=11, replica_groups=mesh['seq'=8,'tile'=4] {'seq'}, use_global_device_ids=true, to_apply=%region_36.37.clone | all-reduce | flops 5120 | bytes 20480
  1290.0 15.2 add_convert_fusion
  1306.0 21.9 %reduce-scatter.38.cloned.1.call-done = bf16[128,3]{1,0:T(8,128)(2,1)} async-done(((bf16[1024,3]{1,0:T(8,128)(2,1)}), bf16[128,3]{1,0:T(8,128)(2,1)}) %reduce-scatter.38.cloned.1.call-update) | async-done | bytes 784
  1328.7 36.3 %reduce-scatter.34.cloned.1.call-done = bf16[128,8]{1,0:T(8,128)(2,1)} async-done(((bf16[1024,8]{1,0:T(8,128)(2,1)}), bf16[128,8]{1,0:T(8,128)(2,1)}) %reduce-scatter.34.cloned.1.call-update) | async-done | bytes 2064
  1365.8 11.9 all-reduce.3
  1380.5 144.3 %all-reduce.7.cloned.1.call-done = (bf16[128,3072]{1,0:T(8,128)(2,1)}, bf16[128,1024]{1,0:T(8,128)(2,1)}, bf16[128,3072]{1,0:T(8,128)(2,1)}, bf16[128,1024]{1,0:...) async-done(((bf16[128,3072]{1,0:T(8,128)(2,1)}, bf16[128,1024]{1,0:T(8,128)(2,1)}, bf16[128,3072]{1,0:T(8,128)(2,1)}, bf16[128,1024]{1,0:T(8,128)(2,1)}, ...) | async-done | bytes 4194320 | tf_op jit(solution)/shard_map/psum | solution.py:329
  (309 shorter events, 371.1 us)
Async XLA Ops:
  7.2 51.0 %all-gather.10.cloned.1.call-start = ((), (), s32[]{:S(2)}) async-start(), calls=%async_computation.11 | async-start | bytes 7077888 | tf_op jit(solution)/shard_map/all_gather | solution.py:87
  7.9 250.6 %all-gather.12.cloned.1.call-start = ((), (), s32[]{:S(2)}) async-start(), calls=%async_computation.12 | async-start | bytes 8519680 | tf_op jit(solution)/shard_map/all_gather | solution.py:125
  40.5 351.8 %copy-start.57 = (f32[1,1024]{1,0:T(1,128)}, f32[1,1024]{1,0:T(1,128)S(1)}, u32[]{:S(2)}) copy-start(f32[1,1024]{1,0:T(1,128)S(1)} %get-tuple-element.52) | copy-start | bytes 12292
  40.5 437.8 %copy-start.55 = (f32[1,1024]{1,0:T(1,128)}, f32[1,1024]{1,0:T(1,128)S(1)}, u32[]{:S(2)}) copy-start(f32[1,1024]{1,0:T(1,128)S(1)} %get-tuple-element.51) | copy-start | bytes 12292
  40.5 351.8 %copy-start.50 = (f32[1,1024]{1,0:T(1,128)}, f32[1,1024]{1,0:T(1,128)S(1)}, u32[]{:S(2)}) copy-start(f32[1,1024]{1,0:T(1,128)S(1)} %get-tuple-element.49) | copy-start | bytes 12292
  68.8 248.4 %all-gather.14.cloned.1.call-start = ((), (), s32[]{:S(2)}) async-start(), calls=%async_computation.13 | async-start | bytes 8519680 | tf_op jit(solution)/shard_map/all_gather | solution.py:124
  69.5 290.2 %all-gather.16.cloned.1.call-start = ((), (), s32[]{:S(2)}) async-start(), calls=%async_computation.14 | async-start | bytes 2359296 | tf_op jit(solution)/shard_map/all_gather | solution.py:88
  70.1 322.2 %all-gather.18.cloned.1.call-start = ((), (), s32[]{:S(2)}) async-start(), calls=%async_computation.15 | async-start | bytes 7077888 | tf_op jit(solution)/shard_map/all_gather | solution.py:89
  70.7 371.9 %all-gather.20.cloned.1.call-start = ((), (), s32[]{:S(2)}) async-start(), calls=%async_computation.16 | async-start | bytes 2359296 | tf_op jit(solution)/shard_map/all_gather | solution.py:90
  70.7 13.7 collective-permute-start
  87.0 47.8 %collective-permute-start.1 = (bf16[1024,1024]{1,0:T(8,128)(2,1)}, bf16[1024,1024]{1,0:T(8,128)(2,1)S(1)}, u32[]{:S(2)}, u32[]{:S(2)}) collective-permute-start(bf16[1024,1024]{1,0:T(8,128)(2,1)} %pad_maximum_fusion.3), channel_id=1, source_target_pairs={{0,24},{4,28},{8,0},{12,4},{16,8},{20,12},{24,16},{28,20},{1,25},{... | collective-permute-start | bytes 6291464 | tf_op jit(solution)/shard_map/ppermute | solution.py:16
  88.3 147.8 %copy-start.62 = (s32[1,13]{1,0:T(1,128)S(1)}, s32[1,13]{1,0:T(1,128)}, u32[]{:S(2)}) copy-start(s32[1,13]{1,0:T(1,128)} %param.17) | copy-start | bytes 160
  88.3 390.0 %all-gather.22.cloned.1.call-start = ((), (), s32[]{:S(2)}) async-start(), calls=%async_computation.17 | async-start | bytes 9437184 | tf_op jit(solution)/shard_map/all_gather | solution.py:91
  138.1 99.5 %collective-permute-start.2 = (bf16[2048,1024]{1,0:T(8,128)(2,1)}, bf16[2048,1024]{1,0:T(8,128)(2,1)}, u32[]{:S(2)}, u32[]{:S(2)}) collective-permute-start(bf16[2048,1024]{1,0:T(8,128)(2,1)} %pad_maximum_fusion.2), channel_id=1, source_target_pairs={{0,16},{4,20},{8,24},{12,28},{16,0},{20,4},{24,8},{28,12},{1,17},{... | collective-permute-start | bytes 12582920 | tf_op jit(solution)/shard_map/ppermute | solution.py:16
  140.5 619.7 %reduce-scatter.20.cloned.1.call-start = ((), (), s32[]{:S(2)}) async-start(), calls=%async_computation.19 | async-start | bytes 8519680 | tf_op jit(solution)/shard_map/reduce_scatter | solution.py:254
  236.0 256.4 %copy-start.52 = (f32[8,1,512]{2,1,0:T(1,128)}, f32[8,1,512]{2,1,0:T(1,128)S(1)}, u32[]{:S(2)}) copy-start(f32[8,1,512]{2,1,0:T(1,128)S(1)} %convert_element_type.288) | copy-start | bytes 49156
  447.8 81.1 %copy-start.18 = (f32[832,1024]{1,0:T(8,128)}, f32[832,1024]{1,0:T(8,128)S(1)}, u32[]{:S(2)}) copy-start(f32[832,1024]{1,0:T(8,128)S(1)} %get-tuple-element.61) | copy-start | bytes 10223620
  640.8 241.5 %reduce-scatter.18.cloned.1.call-start = ((), (), s32[]{:S(2)}) async-start(), calls=%async_computation.18 | async-start | bytes 8519680 | tf_op jit(solution)/shard_map/reduce_scatter | solution.py:251
  679.9 247.9 %reduce-scatter.24.cloned.1.call-start = ((), (), s32[]{:S(2)}) async-start(), calls=%async_computation.21 | async-start | bytes 2359296 | tf_op jit(solution)/shard_map/reduce_scatter | solution.py:299
  687.0 286.3 %reduce-scatter.28.cloned.1.call-start = ((), (), s32[]{:S(2)}) async-start(), calls=%async_computation.23 | async-start | bytes 2359296 | tf_op jit(solution)/shard_map/reduce_scatter | solution.py:305
  693.7 344.6 %reduce-scatter.26.cloned.1.call-start = ((), (), s32[]{:S(2)}) async-start(), calls=%async_computation.22 | async-start | bytes 7077888 | tf_op jit(solution)/shard_map/reduce_scatter | solution.py:302
  705.2 408.3 %reduce-scatter.30.cloned.1.call-start = ((), (), s32[]{:S(2)}) async-start(), calls=%async_computation.24 | async-start | bytes 9437184 | tf_op jit(solution)/shard_map/reduce_scatter | solution.py:308
  721.6 466.5 %reduce-scatter.32.cloned.1.call-start = ((), (), s32[]{:S(2)}) async-start(), calls=%async_computation.25 | async-start | bytes 9437184 | tf_op jit(solution)/shard_map/reduce_scatter | solution.py:311
  740.1 513.4 %reduce-scatter.22.cloned.1.call-start = ((), (), s32[]{:S(2)}) async-start(), calls=%async_computation.20 | async-start | bytes 7077888 | tf_op jit(solution)/shard_map/reduce_scatter | solution.py:296
  893.8 411.4 %reduce-scatter.36.cloned.1.call-start = ((), (), s32[]{:S(2)}) async-start(), calls=%async_computation.27 | async-start | bytes 294912
  909.3 418.6 %reduce-scatter.38.cloned.1.call-start = ((), (), s32[]{:S(2)}) async-start(), calls=%async_computation.28 | async-start | bytes 294912
  915.4 338.1 %copy-start.66 = (bf16[128]{0:T(256)(128)(2,1)S(1)}, bf16[128]{0:T(256)(128)(2,1)}, u32[]{:S(2)}) copy-start(bf16[128]{0:T(256)(128)(2,1)} %param.27) | copy-start | bytes 772
  917.8 346.1 %copy-start.69 = (u32[32]{0:T(128)S(1)}, u32[32]{0:T(128)}, u32[]{:S(2)}) copy-start(u32[32]{0:T(128)} %constant.78) | copy-start | bytes 388
  917.8 348.0 %copy-start.54 = (bf16[4096]{0:T(1024)(128)(2,1)S(1)}, bf16[4096]{0:T(1024)(128)(2,1)}, u32[]{:S(2)}) copy-start(bf16[4096]{0:T(1024)(128)(2,1)} %get-tuple-element.69) | copy-start | bytes 24580
  917.8 372.2 %copy-start.20 = (f32[832,1024]{1,0:T(8,128)S(1)}, f32[832,1024]{1,0:T(8,128)}, u32[]{:S(2)}) copy-start(f32[832,1024]{1,0:T(8,128)} %copy-done.18) | copy-start | bytes 10223620
  917.9 447.1 %reduce-scatter.34.cloned.1.call-start = ((), (), s32[]{:S(2)}) async-start(), calls=%async_computation.26 | async-start | bytes 294912
  919.1 605.8 %all-reduce.7.cloned.1.call-start = ((), (), s32[]{:S(2)}) async-start(), calls=%async_computation.29 | async-start | bytes 8388608 | tf_op jit(solution)/shard_map/psum | solution.py:329
  (62 other events, 632.9 us)
Sparse Core Ops, SparseCore 0:
  9.9 48.2 all-gather.9
  68.9 123.9 all-gather.11
  195.0 122.0 all-gather.13
  318.9 26.0 all-gather.15
  346.7 45.5 all-gather.17
  394.0 27.8 all-gather.19
  423.8 54.3 all-gather.21
  641.0 119.2 reduce-scatter.19
  762.6 119.7 reduce-scatter.17
  886.0 41.7 reduce-scatter.23
  932.0 41.2 reduce-scatter.27
  976.5 61.7 reduce-scatter.25
  1042.2 71.2 reduce-scatter.29
  1116.8 71.2 reduce-scatter.31
  1191.7 61.7 reduce-scatter.21
  1256.9 33.5 reduce-scatter.35
  1294.3 33.5 reduce-scatter.37
  1331.3 33.5 reduce-scatter.33
  1368.0 156.7 all-reduce.6
